TPU v7x, 128 devices: a whole 4x4x4 slice. The times are simulated.
128 devices in a mesh: seq: 32 (over x_hi, z, y), tensor: 2 (over core), dp: 2 (over x_lo).
Axes of the slice: x: 4 (x_hi: 2, x_lo: 2; x = x_hi * 2 + x_lo), y: 4, z: 4, core: 2. Of those that a mesh axis runs over, the one named last changes fastest.
Arguments:
- inputs: bfloat16 [2, 24576, 1536], P('dp', 'seq', 'tensor'), may hold values from -6 to 6
- lengths: int32 [2], P('dp'), may hold values from 6144 to 24576, as said below
- cotangent: bfloat16 [2, 24576, 1536], P('dp', 'seq', 'tensor'), may hold values from -6 to 6
- w_value: bfloat16 [1536, 1536], P(None, 'tensor'), may hold values from -0.15625 to 0.15625
- w_gate: bfloat16 [1536, 1536], P(None, 'tensor'), may hold values from -0.15625 to 0.15625
- kernel: bfloat16 [31, 1536], P(None, 'tensor'), may hold values from -1 to 1
- w_out: bfloat16 [1536, 1536], P('tensor'), may hold values from -0.15625 to 0.15625
Outputs:
- output: bfloat16 [2, 24576, 1536], P('dp', 'seq', 'tensor')
- input_gradient: bfloat16 [2, 24576, 1536], P('dp', 'seq', 'tensor')
- value_grad: float32 [1536, 1536], P(('seq', 'dp'), 'tensor')
- gate_grad: float32 [1536, 1536], P(('seq', 'dp'), 'tensor')
- kernel_grad: float32 [31, 1536], P(None, 'tensor')
- out_grad: float32 [1536, 1536], P('tensor', ('seq', 'dp'))
Inputs may be any that keep to these rules, and one draw needn't show every extreme that they name: `lengths`: in every draw some utterance has all 24576 frames valid.
All inputs are finite; a program needn't handle non-finite values.
Results may differ from a plain program's by a relative error of at most 0.009.
Values may be sent and summed in bfloat16 or wider, within the bound.
A program may use at most 128 MiB of HBM per device.

v0:
```python
import jax
import jax.numpy as jnp
from jax import lax
from jax.sharding import PartitionSpec as P

epsilon = 1e-05


def padded_2(shard, sides, width):
    for axis, dim in sides:
        peers, length = (lax.axis_size(axis), shard.shape[dim])
        up = [(i, (i + 1) % peers) for i in range(peers - 1)]
        down = [(j, i) for i, j in up]
        last = lax.slice_in_dim(shard, length - width, length, axis=dim)
        leading = lax.slice_in_dim(shard, 0, width, axis=dim)
        before = lax.ppermute(last, axis, up)
        after = lax.ppermute(leading, axis, down)
        shard = jnp.concatenate([before, shard, after], axis=dim)
    return shard


def layer_normalizer(values):
    center = values - jnp.mean(values, axis=-1, keepdims=True)
    inverse = lax.rsqrt(jnp.mean(center * center, axis=-1, keepdims=True) + epsilon)
    return (center * inverse, inverse)


def shards(inputs, lengths, cotangent, w_value, w_gate, kernel, w_out):
    frame_total = inputs[0]
    count = frame_total.shape[0]
    channel_total = frame_total.shape[1]
    channel_width = channel_total * lax.axis_size("tensor")
    taps_count = kernel.shape[0]
    half = (taps_count - 1) // 2
    tensor_position = lax.axis_index("tensor")
    first_frame = lax.axis_index("seq") * count
    positions = first_frame + jnp.arange(count, dtype=jnp.int32)
    valid = (positions < lengths[0]).astype(jnp.float32)[:, None]
    taps = kernel.astype(jnp.float32)
    complete_rows = lax.all_gather(frame_total, "tensor", axis=1, tiled=True)
    centered_scaled, inverse_deviation_one = layer_normalizer(complete_rows.astype(jnp.float32))
    normalized_rows = centered_scaled.astype(jnp.bfloat16)
    values = jnp.dot(normalized_rows, w_value, preferred_element_type=jnp.float32)
    gates = jnp.dot(normalized_rows, w_gate, preferred_element_type=jnp.float32)
    sigma = jax.nn.sigmoid(gates)
    hidden = (values * sigma * valid).astype(jnp.bfloat16)
    padded = padded_2(hidden, (("seq", 0),), half).astype(jnp.float32)
    conv = jnp.zeros((count, channel_total), jnp.float32)
    for offset in range(taps_count):
        conv = conv + padded[offset : offset + count] * taps[offset]
    conv_sum, conv_square = lax.psum(
        (jnp.sum(conv, axis=-1), jnp.sum(conv * conv, axis=-1)), "tensor"
    )
    conv_mean = (conv_sum / channel_width)[:, None]
    conv_var = (conv_square / channel_width)[:, None] - conv_mean * conv_mean
    rstd_two = lax.rsqrt(conv_var + epsilon)
    zhat = (conv - conv_mean) * rstd_two
    swish_gate = jax.nn.sigmoid(zhat)
    swished = (zhat * swish_gate).astype(jnp.bfloat16)
    partial_out = jnp.dot(swished, w_out, preferred_element_type=jnp.float32)
    summed = lax.psum_scatter(
        partial_out.astype(jnp.bfloat16), "tensor", scatter_dimension=1, tiled=True
    ).astype(jnp.float32)
    output = (frame_total.astype(jnp.float32) + summed).astype(jnp.bfloat16)
    upstream = cotangent[0]
    upstream_whole = lax.all_gather(upstream, "tensor", axis=1, tiled=True)
    out_term = jnp.dot(swished.T, upstream_whole, preferred_element_type=jnp.float32)
    dswish = jnp.dot(upstream_whole, w_out.T, preferred_element_type=jnp.float32)
    dswish = dswish * (swish_gate + zhat * swish_gate * (1.0 - swish_gate))
    slope_sum, slope_cross = lax.psum(
        (jnp.sum(dswish, axis=-1), jnp.sum(dswish * zhat, axis=-1)), "tensor"
    )
    dconv = rstd_two * (
        dswish
        - (slope_sum / channel_width)[:, None]
        - zhat * (slope_cross / channel_width)[:, None]
    )
    dconv = dconv.astype(jnp.bfloat16)
    slope = dconv.astype(jnp.float32)
    kernel_term = jnp.stack(
        [jnp.sum(padded[offset : offset + count] * slope, axis=0) for offset in range(taps_count)]
    )
    slope_pad = padded_2(dconv, (("seq", 0),), half).astype(jnp.float32)
    dhidden = jnp.zeros((count, channel_total), jnp.float32)
    for offset in range(taps_count):
        dhidden = dhidden + slope_pad[2 * half - offset : 2 * half - offset + count] * taps[offset]
    dhidden = dhidden * valid
    dvalues = (dhidden * sigma).astype(jnp.bfloat16)
    dgates = (dhidden * values * sigma * (1.0 - sigma)).astype(jnp.bfloat16)
    value_term = jnp.dot(normalized_rows.T, dvalues, preferred_element_type=jnp.float32)
    gate_term = jnp.dot(normalized_rows.T, dgates, preferred_element_type=jnp.float32)
    kernel_grad = lax.psum(kernel_term, ("seq", "dp"))
    dnormed_part = jnp.dot(dvalues, w_value.T, preferred_element_type=jnp.float32) + jnp.dot(
        dgates, w_gate.T, preferred_element_type=jnp.float32
    )
    normalized_grad = lax.psum_scatter(
        dnormed_part.astype(jnp.bfloat16), "tensor", scatter_dimension=1, tiled=True
    ).astype(jnp.float32)
    local_centered_scaled = lax.dynamic_slice_in_dim(
        centered_scaled, tensor_position * channel_total, channel_total, 1
    )
    input_total_sum, input_cross_term = lax.psum(
        (
            jnp.sum(normalized_grad, axis=-1),
            jnp.sum(normalized_grad * local_centered_scaled, axis=-1),
        ),
        "tensor",
    )
    input_gradient = upstream.astype(jnp.float32) + inverse_deviation_one * (
        normalized_grad
        - (input_total_sum / channel_width)[:, None]
        - local_centered_scaled * (input_cross_term / channel_width)[:, None]
    )
    input_gradient = input_gradient.astype(jnp.bfloat16)
    value_grad, gate_grad, out_grad = (
        lax.psum_scatter(value_term, ("seq", "dp"), scatter_dimension=0, tiled=True),
        lax.psum_scatter(gate_term, ("seq", "dp"), scatter_dimension=0, tiled=True),
        lax.psum_scatter(out_term, ("seq", "dp"), scatter_dimension=1, tiled=True),
    )
    return (output[None], input_gradient[None], value_grad, gate_grad, kernel_grad, out_grad)


def solution(mesh):
    return jax.shard_map(
        shards,
        mesh=mesh,
        in_specs=(
            P("dp", "seq", "tensor"),
            P("dp"),
            P("dp", "seq", "tensor"),
            P(None, "tensor"),
            P(None, "tensor"),
            P(None, "tensor"),
            P("tensor", None),
        ),
        out_specs=(
            P("dp", "seq", "tensor"),
            P("dp", "seq", "tensor"),
            P(("seq", "dp"), "tensor"),
            P(("seq", "dp"), "tensor"),
            P(None, "tensor"),
            P("tensor", ("seq", "dp")),
        ),
        check_vma=False,
    )
```

profile of v0, /device:TPU:0, one launch (start us, length us, event | category | flops | bytes accessed | tf_op | source)
XLA Modules:
  0.0 1369.6 jit_solution(1484095070607599668)
XLA Ops:
  7.2 0.0 copy-start
  7.2 0.0 all-gather.5.cloned.1.call-start
  7.2 0.7 all-gather.5.cloned.1.call-update
  7.9 0.0 all-gather.7.cloned.1.call-start
  8.0 0.7 all-gather.7.cloned.1.call-update
  8.7 0.0 reduce-scatter.6.cloned.1.call-start
  9.4 0.2 slice_reduce_fusion.30
  9.8 16.1 %all-gather.5.cloned.1.call-done = bf16[1,768,1536]{2,1,0:T(8,128)(2,1)} async-done(((bf16[1,768,768]{2,1,0:T(8,128)(2,1)}), bf16[1,768,1536]{2,1,0:T(8,128)(2,1)}) %all-gather.5.cloned.1.call-update) | async-done | bytes 2359312 | tf_op jit(solution)/shard_map/all_gather | solution.py:40
  25.8 2.2 convert_reduce_fusion
  28.0 0.2 copy-done.2
  28.2 0.8 fusion.3
  29.0 2.3 add_divide_fusion.1
  31.4 3.5 multiply_convert_fusion.3
  34.9 3.5 collective-permute-start
  38.4 1.3 collective-permute-start.1
  39.7 0.1 slice_reduce_fusion.29
  39.9 4.2 collective-permute-done.1
  44.1 0.2 maximum_convert_fusion
  44.5 10.7 fusion.94
  55.4 2.5 all-reduce.2
  57.9 0.0 all-gather.7.cloned.1.call-done
  57.9 7.0 fusion.93
  64.9 2.5 all-reduce.1
  67.5 27.0 %fusion.39 = (f32[768]{0:T(1024)}, f32[768]{0:T(1024)}, f32[768]{0:T(1024)}, f32[768]{0:T(1024)}, f32[768]{0:T(1024)}, /*index=5*/f32[768]{0:T(1024)}, f32[768]{...) fusion(f32[798,768]{1,0:T(8,128)} %copy-done.1, ...), kind=kLoop, calls=%fused_computation.77 | loop fusion | flops 25938432 | bytes 48433152 | tf_op jit(solution)/shard_map/reduce_sum | solution.py:81
  94.5 0.6 fusion.96
  95.1 4.0 collective-permute-start.2
  99.0 1.3 collective-permute-start.3
  100.4 3.9 convolution_convert_fusion
  104.3 0.0 reduce-scatter.6.cloned.1.call-update
  104.3 0.0 reduce-scatter.8.cloned.1.call-start
  104.6 0.4 collective-permute-done.3
  105.1 1.1 maximum_convert_fusion.1
  106.5 10.9 multiply_convert_fusion
  117.4 0.4 multiply_convert_fusion.1
  117.8 2.0 fusion.98
  119.8 0.1 copy-done.97
  119.9 3.5 add_convert_fusion
  123.5 0.0 reduce-scatter.8.cloned.1.call-update
  123.5 0.3 all-reduce.5.cloned.1.call-start
  123.9 15.4 %fusion.38 = (f32[768]{0:T(1024)S(1)}, f32[768]{0:T(1024)S(1)}, f32[768]{0:T(1024)S(1)}, f32[768]{0:T(1024)S(1)}, f32[768]{0:T(1024)S(1)}, /*index=5*/f32[768]{0...) fusion(bf16[768,768]{1,0:T(8,128)(2,1)S(1)} %get-tuple-element., ...), kind=kLoop, calls=%fused_computation.76 | loop fusion | flops 15915264 | bytes 31890432 | tf_op jit(solution)/shard_map/reduce_sum | solution.py:81
  139.9 2.6 stack.127
  142.5 0.0 all-reduce.5.cloned.1.call-update
  142.5 0.0 reduce-scatter.14.cloned.1.call-start
  142.6 7.1 fusion.72
  149.7 0.0 reduce-scatter.14.cloned.1.call-update
  149.8 0.0 reduce-scatter.10.cloned.1.call-start
  149.8 1.2 copy-done.9
  151.0 6.1 fusion.88
  157.1 0.0 reduce-scatter.10.cloned.1.call-update
  157.1 0.0 reduce-scatter.12.cloned.1.call-start
  157.1 1.2 copy-done.11
  158.3 6.1 fusion.86
  164.5 0.0 reduce-scatter.12.cloned.1.call-update
  164.5 4.4 fusion.1
  169.0 2.6 fusion.80
  171.6 2.6 convert_reduce_fusion.1
  174.2 3.1 all-reduce
  177.2 0.7 broadcast_multiply_fusion
  177.9 3.6 fusion.81
  181.6 95.1 %all-reduce.5.cloned.1.call-done = f32[31,768]{1,0:T(8,128)} async-done(((f32[31,768]{1,0:T(8,128)}), f32[31,768]{1,0:T(8,128)}) %all-reduce.5.cloned.1.call-update) | async-done | bytes 95248 | tf_op jit(solution)/shard_map/psum | solution.py:92
  276.7 363.2 %reduce-scatter.14.cloned.1.call-done = f32[768,24]{0,1:T(8,128)} async-done(((f32[768,1536]{0,1:T(8,128)}), f32[768,24]{0,1:T(8,128)}) %reduce-scatter.14.cloned.1.call-update) | async-done | bytes 73744 | tf_op jit(solution)/shard_map/reduce_scatter | solution.py:118
  639.9 360.7 %reduce-scatter.10.cloned.1.call-done = f32[24,768]{1,0:T(8,128)} async-done(((f32[1536,768]{1,0:T(8,128)}), f32[24,768]{1,0:T(8,128)}) %reduce-scatter.10.cloned.1.call-update) | async-done | bytes 73744 | tf_op jit(solution)/shard_map/reduce_scatter | solution.py:116
  1000.6 360.6 %reduce-scatter.12.cloned.1.call-done = f32[24,768]{1,0:T(8,128)} async-done(((f32[1536,768]{1,0:T(8,128)}), f32[24,768]{1,0:T(8,128)}) %reduce-scatter.12.cloned.1.call-update) | async-done | bytes 73744 | tf_op jit(solution)/shard_map/reduce_scatter | solution.py:117
  1361.2 1.5 copy.15
  (234 shorter events, 0.6 us)
Async XLA Ops:
  7.2 24.2 %copy-start = (bf16[1536,768]{1,0:T(8,128)(2,1)S(1)}, bf16[1536,768]{1,0:T(8,128)(2,1)}, u32[]{:S(2)}) copy-start(bf16[1536,768]{1,0:T(8,128)(2,1)} %param.10) | copy-start | bytes 7077892
  7.2 18.6 %all-gather.5.cloned.1.call-start = ((), (), s32[]{:S(2)}) async-start(), calls=%async_computation.11 | async-start | bytes 3538944 | tf_op jit(solution)/shard_map/all_gather | solution.py:40
  7.9 50.0 %all-gather.7.cloned.1.call-start = ((), (), s32[]{:S(2)}) async-start(), calls=%async_computation.12 | async-start | bytes 3538944 | tf_op jit(solution)/shard_map/all_gather | solution.py:66
  8.7 160.3 %reduce-scatter.6.cloned.1.call-start = ((), (), s32[]{:S(2)}) async-start(), calls=%async_computation.5 | async-start | bytes 3538944 | tf_op jit(solution)/shard_map/reduce_scatter | solution.py:61
  9.6 34.8 %copy-start.13 = (f32[768]{0:T(1024)}, f32[768]{0:T(1024)S(1)}, u32[]{:S(2)}) copy-start(f32[768]{0:T(1024)S(1)} %get-tuple-element.47) | copy-start | bytes 9220
  9.6 34.8 %copy-start.15 = (f32[768]{0:T(1024)}, f32[768]{0:T(1024)S(1)}, u32[]{:S(2)}) copy-start(f32[768]{0:T(1024)S(1)} %get-tuple-element.48) | copy-start | bytes 9220
  9.6 34.8 %copy-start.17 = (f32[768]{0:T(1024)}, f32[768]{0:T(1024)S(1)}, u32[]{:S(2)}) copy-start(f32[768]{0:T(1024)S(1)} %get-tuple-element.49) | copy-start | bytes 9220
  9.6 34.8 %copy-start.19 = (f32[768]{0:T(1024)}, f32[768]{0:T(1024)S(1)}, u32[]{:S(2)}) copy-start(f32[768]{0:T(1024)S(1)} %get-tuple-element.50) | copy-start | bytes 9220
  9.6 34.8 %copy-start.21 = (f32[768]{0:T(1024)}, f32[768]{0:T(1024)S(1)}, u32[]{:S(2)}) copy-start(f32[768]{0:T(1024)S(1)} %get-tuple-element.51) | copy-start | bytes 9220
  9.6 34.8 %copy-start.23 = (f32[768]{0:T(1024)}, f32[768]{0:T(1024)S(1)}, u32[]{:S(2)}) copy-start(f32[768]{0:T(1024)S(1)} %get-tuple-element.52) | copy-start | bytes 9220
  9.6 34.8 %copy-start.25 = (f32[768]{0:T(1024)}, f32[768]{0:T(1024)S(1)}, u32[]{:S(2)}) copy-start(f32[768]{0:T(1024)S(1)} %get-tuple-element.53) | copy-start | bytes 9220
  9.6 34.8 %copy-start.27 = (f32[768]{0:T(1024)}, f32[768]{0:T(1024)S(1)}, u32[]{:S(2)}) copy-start(f32[768]{0:T(1024)S(1)} %get-tuple-element.54) | copy-start | bytes 9220
  9.7 34.8 %copy-start.29 = (f32[768]{0:T(1024)}, f32[768]{0:T(1024)S(1)}, u32[]{:S(2)}) copy-start(f32[768]{0:T(1024)S(1)} %get-tuple-element.55) | copy-start | bytes 9220
  9.7 34.8 %copy-start.31 = (f32[768]{0:T(1024)}, f32[768]{0:T(1024)S(1)}, u32[]{:S(2)}) copy-start(f32[768]{0:T(1024)S(1)} %get-tuple-element.56) | copy-start | bytes 9220
  9.7 34.8 %copy-start.33 = (f32[768]{0:T(1024)}, f32[768]{0:T(1024)S(1)}, u32[]{:S(2)}) copy-start(f32[768]{0:T(1024)S(1)} %get-tuple-element.57) | copy-start | bytes 9220
  9.7 34.8 %copy-start.35 = (f32[768]{0:T(1024)}, f32[768]{0:T(1024)S(1)}, u32[]{:S(2)}) copy-start(f32[768]{0:T(1024)S(1)} %get-tuple-element.58) | copy-start | bytes 9220
  9.7 34.8 %copy-start.37 = (f32[768]{0:T(1024)}, f32[768]{0:T(1024)S(1)}, u32[]{:S(2)}) copy-start(f32[768]{0:T(1024)S(1)} %get-tuple-element.59) | copy-start | bytes 9220
  9.7 34.8 %copy-start.39 = (f32[768]{0:T(1024)}, f32[768]{0:T(1024)S(1)}, u32[]{:S(2)}) copy-start(f32[768]{0:T(1024)S(1)} %get-tuple-element.60) | copy-start | bytes 9220
  9.7 34.8 %copy-start.41 = (f32[768]{0:T(1024)}, f32[768]{0:T(1024)S(1)}, u32[]{:S(2)}) copy-start(f32[768]{0:T(1024)S(1)} %get-tuple-element.61) | copy-start | bytes 9220
  9.7 21.6 %copy-start.71 = (f32[768]{0:T(1024)}, f32[768]{0:T(1024)S(1)}, u32[]{:S(2)}) copy-start(f32[768]{0:T(1024)S(1)} %fusion.82) | copy-start | bytes 9220
  34.9 5.0 collective-permute-start
  38.4 5.7 collective-permute-start.1
  39.8 15.5 %copy-start.45 = (f32[768]{0:T(1024)}, f32[768]{0:T(1024)S(1)}, u32[]{:S(2)}) copy-start(f32[768]{0:T(1024)S(1)} %get-tuple-element.62) | copy-start | bytes 9220
  39.8 15.5 %copy-start.47 = (f32[768]{0:T(1024)}, f32[768]{0:T(1024)S(1)}, u32[]{:S(2)}) copy-start(f32[768]{0:T(1024)S(1)} %get-tuple-element.63) | copy-start | bytes 9220
  39.8 15.5 %copy-start.49 = (f32[768]{0:T(1024)}, f32[768]{0:T(1024)S(1)}, u32[]{:S(2)}) copy-start(f32[768]{0:T(1024)S(1)} %get-tuple-element.64) | copy-start | bytes 9220
  39.8 15.5 %copy-start.51 = (f32[768]{0:T(1024)}, f32[768]{0:T(1024)S(1)}, u32[]{:S(2)}) copy-start(f32[768]{0:T(1024)S(1)} %get-tuple-element.65) | copy-start | bytes 9220
  39.8 15.5 %copy-start.53 = (f32[768]{0:T(1024)}, f32[768]{0:T(1024)S(1)}, u32[]{:S(2)}) copy-start(f32[768]{0:T(1024)S(1)} %get-tuple-element.66) | copy-start | bytes 9220
  39.8 15.5 %copy-start.55 = (f32[768]{0:T(1024)}, f32[768]{0:T(1024)S(1)}, u32[]{:S(2)}) copy-start(f32[768]{0:T(1024)S(1)} %get-tuple-element.67) | copy-start | bytes 9220
  39.8 15.5 %copy-start.57 = (f32[768]{0:T(1024)}, f32[768]{0:T(1024)S(1)}, u32[]{:S(2)}) copy-start(f32[768]{0:T(1024)S(1)} %get-tuple-element.68) | copy-start | bytes 9220
  39.9 15.5 %copy-start.59 = (f32[768]{0:T(1024)}, f32[768]{0:T(1024)S(1)}, u32[]{:S(2)}) copy-start(f32[768]{0:T(1024)S(1)} %get-tuple-element.69) | copy-start | bytes 9220
  39.9 15.5 %copy-start.61 = (f32[768]{0:T(1024)}, f32[768]{0:T(1024)S(1)}, u32[]{:S(2)}) copy-start(f32[768]{0:T(1024)S(1)} %get-tuple-element.70) | copy-start | bytes 9220
  39.9 15.5 %copy-start.63 = (f32[768]{0:T(1024)}, f32[768]{0:T(1024)S(1)}, u32[]{:S(2)}) copy-start(f32[768]{0:T(1024)S(1)} %get-tuple-element.71) | copy-start | bytes 9220
  39.9 15.5 %copy-start.65 = (f32[768]{0:T(1024)}, f32[768]{0:T(1024)S(1)}, u32[]{:S(2)}) copy-start(f32[768]{0:T(1024)S(1)} %get-tuple-element.72) | copy-start | bytes 9220
  39.9 15.5 %copy-start.67 = (f32[768]{0:T(1024)}, f32[768]{0:T(1024)S(1)}, u32[]{:S(2)}) copy-start(f32[768]{0:T(1024)S(1)} %get-tuple-element.73) | copy-start | bytes 9220
  44.3 11.0 copy-start.1
  67.4 32.9 %copy-start.3 = (f32[768,768]{1,0:T(8,128)S(1)}, f32[768,768]{1,0:T(8,128)}, u32[]{:S(2)}) copy-start(f32[768,768]{1,0:T(8,128)} %get-tuple-element.83) | copy-start | bytes 7077892
  67.4 32.9 %copy-start.92 = (f32[768]{0:T(1024)S(1)}, f32[768]{0:T(1024)}, u32[]{:S(2)}) copy-start(f32[768]{0:T(1024)} %copy-done.91) | copy-start | bytes 9220
  67.4 32.9 %copy-start.94 = (f32[768]{0:T(1024)S(1)}, f32[768]{0:T(1024)}, u32[]{:S(2)}) copy-start(f32[768]{0:T(1024)} %copy-done.93) | copy-start | bytes 9220
  67.4 32.9 %copy-start.95 = (bf16[768,1536]{1,0:T(8,128)(2,1)S(1)}, bf16[768,1536]{1,0:T(8,128)(2,1)}, u32[]{:S(2)}) copy-start(bf16[768,1536]{1,0:T(8,128)(2,1)} %param.13) | copy-start | bytes 7077892
  95.1 9.5 collective-permute-start.2
  99.0 6.0 collective-permute-start.3
  104.3 67.3 %reduce-scatter.8.cloned.1.call-start = ((), (), s32[]{:S(2)}) async-start(), calls=%async_computation.6 | async-start | bytes 3538944 | tf_op jit(solution)/shard_map/reduce_scatter | solution.py:96
  123.5 16.4 %copy-start.76 = (f32[768]{0:T(1024)S(1)}, f32[768]{0:T(1024)}, u32[]{:S(2)}) copy-start(f32[768]{0:T(1024)} %get-tuple-element.6) | copy-start | bytes 9220
  123.5 16.4 %copy-start.75 = (f32[768]{0:T(1024)S(1)}, f32[768]{0:T(1024)}, u32[]{:S(2)}) copy-start(f32[768]{0:T(1024)} %get-tuple-element.7) | copy-start | bytes 9220
  123.5 16.4 %copy-start.74 = (f32[768]{0:T(1024)S(1)}, f32[768]{0:T(1024)}, u32[]{:S(2)}) copy-start(f32[768]{0:T(1024)} %get-tuple-element.8) | copy-start | bytes 9220
  123.5 16.4 %copy-start.73 = (f32[768]{0:T(1024)S(1)}, f32[768]{0:T(1024)}, u32[]{:S(2)}) copy-start(f32[768]{0:T(1024)} %get-tuple-element.9) | copy-start | bytes 9220
  123.5 153.2 %all-reduce.5.cloned.1.call-start = ((), (), s32[]{:S(2)}) async-start(), calls=%async_computation.9 | async-start | bytes 196608 | tf_op jit(solution)/shard_map/psum | solution.py:92
  123.8 15.7 %copy-start.90 = (f32[768]{0:T(1024)S(1)}, f32[768]{0:T(1024)}, u32[]{:S(2)}) copy-start(f32[768]{0:T(1024)} %get-tuple-element.10) | copy-start | bytes 9220
  123.8 15.8 %copy-start.89 = (f32[768]{0:T(1024)S(1)}, f32[768]{0:T(1024)}, u32[]{:S(2)}) copy-start(f32[768]{0:T(1024)} %get-tuple-element.11) | copy-start | bytes 9220
  123.8 15.8 %copy-start.88 = (f32[768]{0:T(1024)S(1)}, f32[768]{0:T(1024)}, u32[]{:S(2)}) copy-start(f32[768]{0:T(1024)} %get-tuple-element.12) | copy-start | bytes 9220
  123.8 15.8 %copy-start.87 = (f32[768]{0:T(1024)S(1)}, f32[768]{0:T(1024)}, u32[]{:S(2)}) copy-start(f32[768]{0:T(1024)} %get-tuple-element.13) | copy-start | bytes 9220
  123.8 15.8 %copy-start.86 = (f32[768]{0:T(1024)S(1)}, f32[768]{0:T(1024)}, u32[]{:S(2)}) copy-start(f32[768]{0:T(1024)} %get-tuple-element.14) | copy-start | bytes 9220
  123.8 15.8 %copy-start.85 = (f32[768]{0:T(1024)S(1)}, f32[768]{0:T(1024)}, u32[]{:S(2)}) copy-start(f32[768]{0:T(1024)} %get-tuple-element.15) | copy-start | bytes 9220
  123.8 15.8 %copy-start.84 = (f32[768]{0:T(1024)S(1)}, f32[768]{0:T(1024)}, u32[]{:S(2)}) copy-start(f32[768]{0:T(1024)} %get-tuple-element.16) | copy-start | bytes 9220
  123.9 15.8 %copy-start.83 = (f32[768]{0:T(1024)S(1)}, f32[768]{0:T(1024)}, u32[]{:S(2)}) copy-start(f32[768]{0:T(1024)} %get-tuple-element.17) | copy-start | bytes 9220
  123.9 15.8 %copy-start.82 = (f32[768]{0:T(1024)S(1)}, f32[768]{0:T(1024)}, u32[]{:S(2)}) copy-start(f32[768]{0:T(1024)} %get-tuple-element.18) | copy-start | bytes 9220
  123.9 15.8 %copy-start.81 = (f32[768]{0:T(1024)S(1)}, f32[768]{0:T(1024)}, u32[]{:S(2)}) copy-start(f32[768]{0:T(1024)} %get-tuple-element.19) | copy-start | bytes 9220
  123.9 15.9 %copy-start.80 = (f32[768]{0:T(1024)S(1)}, f32[768]{0:T(1024)}, u32[]{:S(2)}) copy-start(f32[768]{0:T(1024)} %get-tuple-element.20) | copy-start | bytes 9220
  123.9 15.9 %copy-start.79 = (f32[768]{0:T(1024)S(1)}, f32[768]{0:T(1024)}, u32[]{:S(2)}) copy-start(f32[768]{0:T(1024)} %get-tuple-element.21) | copy-start | bytes 9220
  123.9 15.9 %copy-start.78 = (f32[768]{0:T(1024)S(1)}, f32[768]{0:T(1024)}, u32[]{:S(2)}) copy-start(f32[768]{0:T(1024)} %get-tuple-element.22) | copy-start | bytes 9220
  123.9 15.9 %copy-start.77 = (f32[768]{0:T(1024)S(1)}, f32[768]{0:T(1024)}, u32[]{:S(2)}) copy-start(f32[768]{0:T(1024)} %get-tuple-element.23) | copy-start | bytes 9220
  142.5 497.4 %reduce-scatter.14.cloned.1.call-start = ((), (), s32[]{:S(2)}) async-start(), calls=%async_computation.10 | async-start | bytes 4792320 | tf_op jit(solution)/shard_map/reduce_scatter | solution.py:118
  149.8 850.8 %reduce-scatter.10.cloned.1.call-start = ((), (), s32[]{:S(2)}) async-start(), calls=%async_computation.7 | async-start | bytes 4792320 | tf_op jit(solution)/shard_map/reduce_scatter | solution.py:116
  157.1 1204.1 %reduce-scatter.12.cloned.1.call-start = ((), (), s32[]{:S(2)}) async-start(), calls=%async_computation.8 | async-start | bytes 4792320 | tf_op jit(solution)/shard_map/reduce_scatter | solution.py:117
  (46 other events, 106.6 us)
Sparse Core Ops, SparseCore 0:
  9.7 16.1 all-gather.4
  27.5 14.9 all-gather.6
  104.4 19.5 reduce-scatter.5
  126.2 18.9 reduce-scatter.7
  150.3 126.3 all-reduce.4
  279.5 360.3 reduce-scatter.13
  642.9 357.6 reduce-scatter.9
  1003.5 357.6 reduce-scatter.11
where the time goes:
time: 1370 us
  waiting for transfers between devices  1200 us (88%)
  other arithmetic  82.8 us (6%)
  matrix products  41.6 us (3%)
  between operations  16.6 us (1%)
    reduce_scatter x1, waiting for transfers between devices, shards(): lax.psum_scatter(out_term, ('seq', 'dp'), scatter_dimension=1, tiled=True)  363 us
    reduce_scatter x1, waiting for transfers between devices, shards(): lax.psum_scatter(value_term, ('seq', 'dp'), scatter_dimension=0, tiled=True)  361 us
    reduce_scatter x1, waiting for transfers between devices, shards(): lax.psum_scatter(gate_term, ('seq', 'dp'), scatter_dimension=0, tiled=True)  361 us
    psum x1, waiting for transfers between devices, shards(): kernel_grad = lax.psum(kernel_term, ('seq', 'dp'))  95.1 us
    reduce_sum x2, other arithmetic, shards(): jnp.sum(padded[offset:offset + count] * slope, axis=0)  42.4 us
  transfers between devices with their start and end apart: 12, of which 7 were waited for; matrix products, arithmetic and copies ran while one was open for 7% of the time, Pallas kernels for 0%

commit v1 on v0

--- a/solution.py
+++ b/solution.py
@@ -4,6 +4,7 @@
 from jax.sharding import PartitionSpec as P
 
 epsilon = 1e-05
+outputs_wrap = lambda page: lax.psum(lax.psum(page, axis_name="dp"), "seq")
 
 
 def padded_2(shard, sides, width):
@@ -89,7 +90,7 @@
     dgates = (dhidden * values * sigma * (1.0 - sigma)).astype(jnp.bfloat16)
     value_term = jnp.dot(normalized_rows.T, dvalues, preferred_element_type=jnp.float32)
     gate_term = jnp.dot(normalized_rows.T, dgates, preferred_element_type=jnp.float32)
-    kernel_grad = lax.psum(kernel_term, ("seq", "dp"))
+    kernel_grad = outputs_wrap(kernel_term)
     dnormed_part = jnp.dot(dvalues, w_value.T, preferred_element_type=jnp.float32) + jnp.dot(
         dgates, w_gate.T, preferred_element_type=jnp.float32
     )

time: 1370 us -> 1600 us (1.17)
  waiting for transfers between devices: 1200 us -> 1420 us
  local copies, waits for them, and re-layouts: 8.21 us -> 30.4 us
    psum x1 -> x2, waiting for transfers between devices: 95.1 us -> 315 us  [outputs_wrap = lambda page: lax.psum(lax.psum(page, axis_name='dp'), 'seq')]
    another operation x32, local copies, waits for them, and re-layouts: 2.72 us -> 23.7 us  [shards(): jnp.stack([jnp.sum(padded[offset:offset + count] * slope, axis=0) for off...]
  transfers between devices with their start and end apart: 12 -> 13, of which waited for: 7 -> 8; matrix products, arithmetic and copies ran while one was open for 7% -> 5% of each run, Pallas kernels for 0% -> 0%
where the time goes in v1:
time: 1600 us
  waiting for transfers between devices  1420 us (89%)
  other arithmetic  70.5 us (4%)
  matrix products  43.8 us (3%)
  local copies, waits for them, and re-layouts  30.4 us (2%)
    reduce_scatter x1, waiting for transfers between devices, shards(): lax.psum_scatter(out_term, ('seq', 'dp'), scatter_dimension=1, tiled=True)  365 us
    reduce_scatter x1, waiting for transfers between devices, shards(): lax.psum_scatter(gate_term, ('seq', 'dp'), scatter_dimension=0, tiled=True)  361 us
    reduce_scatter x1, waiting for transfers between devices, shards(): lax.psum_scatter(value_term, ('seq', 'dp'), scatter_dimension=0, tiled=True)  361 us
    psum x2, waiting for transfers between devices, outputs_wrap = lambda page: lax.psum(lax.psum(page, axis_name='dp'), 'seq')  315 us
  transfers between devices with their start and end apart: 13, of which 8 were waited for; matrix products, arithmetic and copies ran while one was open for 5% of the time, Pallas kernels for 0%

profile of v1, /device:TPU:0, one launch (start us, length us, event | category | flops | bytes accessed | tf_op | source)
XLA Modules:
  0.0 1603.9 jit_solution(10749047523685592035)
XLA Ops:
  7.2 0.7 all-gather.5.cloned.1.call-update
  8.0 0.7 all-gather.7.cloned.1.call-update
  9.4 0.7 slice_reduce_fusion.30
  10.2 0.6 fusion.82
  10.8 15.1 all-gather.5.cloned.1.call-done
  25.8 2.2 convert_reduce_fusion
  28.2 0.8 fusion.3
  29.0 2.3 add_divide_fusion.1
  31.4 3.6 multiply_convert_fusion.3
  35.1 3.5 collective-permute-start
  38.6 1.3 collective-permute-start.1
  39.9 1.2 slice_reduce_fusion.29
  41.2 3.1 collective-permute-done.1
  44.7 10.8 fusion.94
  55.6 2.5 all-reduce.2
  58.2 7.0 fusion.93
  65.2 2.5 all-reduce.1
  67.7 25.7 %fusion.39 = (f32[768]{0:T(1024)S(1)}, f32[768]{0:T(1024)S(1)}, f32[768]{0:T(1024)S(1)}, f32[768]{0:T(1024)S(1)}, f32[768]{0:T(1024)S(1)}, /*index=5*/f32[768]{0...) fusion(f32[798,768]{1,0:T(8,128)} %copy-done.1, ...), kind=kLoop, calls=%fused_computation.77 | loop fusion | flops 25938432 | bytes 48433152 | tf_op jit(solution)/shard_map/reduce_sum | solution.py:82
  93.4 3.9 fusion.38
  97.2 0.6 fusion.96
  97.9 0.6 stack.114
  98.5 0.6 stack.115
  99.0 0.6 stack.116
  100.8 0.6 stack.119
  101.4 0.6 stack.120
  102.0 0.6 stack.121
  102.6 0.6 stack.122
  104.9 0.6 stack.96
  106.1 0.6 stack.101
  107.3 0.6 stack.103
  109.0 0.6 stack.106
  110.2 0.6 stack.108
  110.8 0.6 stack.109
  111.4 0.6 stack.110
  112.0 0.6 stack.111
  113.2 0.6 stack.113
  113.8 0.6 stack.126
  114.4 0.6 stack.97
  116.1 5.4 stack.127
  121.6 4.0 collective-permute-start.2
  125.6 1.3 collective-permute-start.3
  126.9 6.3 convolution_convert_fusion
  133.6 1.1 maximum_convert_fusion.1
  135.2 10.9 multiply_convert_fusion
  146.5 2.0 fusion.98
  148.5 3.6 add_convert_fusion
  152.4 2.3 all-reduce.6.cloned.1.call-done
  154.8 6.8 fusion.72
  161.7 0.6 copy-done.43
  162.3 6.1 fusion.88
  168.5 1.3 copy-done.9
  169.7 6.3 fusion.86
  176.0 4.4 fusion.1
  180.5 2.6 fusion.80
  183.0 4.0 reduce-scatter.8.cloned.1.call-done
  187.0 2.5 convert_reduce_fusion.1
  189.5 3.1 all-reduce
  192.6 0.7 broadcast_multiply_fusion
  193.3 3.6 fusion.81
  196.9 312.4 %all-reduce.8.cloned.1.call-done = f32[31,768]{1,0:T(8,128)} async-done(((f32[31,768]{1,0:T(8,128)}), f32[31,768]{1,0:T(8,128)}) %all-reduce.8.cloned.1.call-update) | async-done | bytes 95248 | tf_op jit(solution)/shard_map/psum | solution.py:7
  509.3 364.8 %reduce-scatter.14.cloned.1.call-done = f32[768,24]{0,1:T(8,128)} async-done(((f32[768,1536]{0,1:T(8,128)}), f32[768,24]{0,1:T(8,128)}) %reduce-scatter.14.cloned.1.call-update) | async-done | bytes 73744 | tf_op jit(solution)/shard_map/reduce_scatter | solution.py:119
  874.1 360.9 %reduce-scatter.10.cloned.1.call-done = f32[24,768]{1,0:T(8,128)} async-done(((f32[1536,768]{1,0:T(8,128)}), f32[24,768]{1,0:T(8,128)}) %reduce-scatter.10.cloned.1.call-update) | async-done | bytes 73744 | tf_op jit(solution)/shard_map/reduce_scatter | solution.py:117
  1235.0 360.9 %reduce-scatter.12.cloned.1.call-done = f32[24,768]{1,0:T(8,128)} async-done(((f32[1536,768]{1,0:T(8,128)}), f32[24,768]{1,0:T(8,128)}) %reduce-scatter.12.cloned.1.call-update) | async-done | bytes 73744 | tf_op jit(solution)/shard_map/reduce_scatter | solution.py:118
  1595.9 1.5 copy.16
  (197 shorter events, 9.7 us)
Async XLA Ops:
  7.2 24.2 %copy-start = (bf16[1536,768]{1,0:T(8,128)(2,1)S(1)}, bf16[1536,768]{1,0:T(8,128)(2,1)}, u32[]{:S(2)}) copy-start(bf16[1536,768]{1,0:T(8,128)(2,1)} %param.10) | copy-start | bytes 7077892
  7.2 2.2 copy-start.11
  7.2 18.6 %all-gather.5.cloned.1.call-start = ((), (), s32[]{:S(2)}) async-start(), calls=%async_computation.12 | async-start | bytes 3538944 | tf_op jit(solution)/shard_map/all_gather | solution.py:41
  7.9 50.2 %all-gather.7.cloned.1.call-start = ((), (), s32[]{:S(2)}) async-start(), calls=%async_computation.13 | async-start | bytes 3538944 | tf_op jit(solution)/shard_map/all_gather | solution.py:67
  8.7 146.1 %all-reduce.6.cloned.1.call-start = ((), (), s32[]{:S(2)}) async-start(), calls=%async_computation.9 | async-start | bytes 196608 | tf_op jit(solution)/shard_map/psum | solution.py:7
  9.4 19.5 %copy-start.10 = (f32[31,768]{1,0:T(8,128)}, f32[31,768]{1,0:T(8,128)S(1)}, u32[]{:S(2)}) copy-start(f32[31,768]{1,0:T(8,128)S(1)} %convert_element_type.70) | copy-start | bytes 285700
  25.8 2.4 copy-start.3
  25.8 3.1 copy-start.76
  28.2 3.1 copy-start.42
  29.0 2.4 copy-start.68
  29.0 2.4 copy-start.70
  31.4 3.6 copy-start.4
  35.0 9.6 copy-start.12
  35.0 9.6 copy-start.14
  35.0 9.6 copy-start.16
  35.0 9.6 copy-start.18
  35.0 9.6 copy-start.20
  35.0 9.6 copy-start.22
  35.0 9.6 copy-start.24
  35.0 9.6 copy-start.26
  35.0 9.6 copy-start.28
  35.0 9.6 copy-start.30
  35.0 9.6 copy-start.32
  35.0 9.6 copy-start.34
  35.0 9.6 copy-start.36
  35.1 9.6 copy-start.38
  35.1 9.6 copy-start.40
  35.1 6.1 collective-permute-start
  38.6 5.7 collective-permute-start.1
  41.1 14.4 copy-start.44
  41.1 14.4 copy-start.46
  41.1 14.4 copy-start.48
  41.1 14.4 copy-start.50
  41.1 14.4 copy-start.52
  41.1 14.4 copy-start.54
  41.2 14.4 copy-start.56
  41.2 14.4 copy-start.58
  41.2 14.4 copy-start.60
  41.2 14.4 copy-start.62
  41.2 14.4 copy-start.64
  41.2 14.4 copy-start.66
  44.6 11.0 copy-start.1
  58.1 7.0 copy-start.72
  58.1 7.0 copy-start.74
  67.6 25.7 %copy-start.2 = (f32[798,768]{1,0:T(8,128)S(1)}, f32[798,768]{1,0:T(8,128)}, u32[]{:S(2)}) copy-start(f32[798,768]{1,0:T(8,128)} %copy-done.1) | copy-start | bytes 7354372
  121.6 58.9 %reduce-scatter.6.cloned.1.call-start = ((), (), s32[]{:S(2)}) async-start(), calls=%async_computation.5 | async-start | bytes 3538944 | tf_op jit(solution)/shard_map/reduce_scatter | solution.py:62
  121.6 11.9 collective-permute-start.2
  125.6 7.9 collective-permute-start.3
  133.2 53.8 %reduce-scatter.8.cloned.1.call-start = ((), (), s32[]{:S(2)}) async-start(), calls=%async_computation.6 | async-start | bytes 3538944 | tf_op jit(solution)/shard_map/reduce_scatter | solution.py:97
  133.2 1.7 copy-start.5
  133.2 1.7 copy-start.13
  133.3 1.7 copy-start.15
  133.3 1.7 copy-start.17
  133.3 1.6 copy-start.19
  146.1 2.4 copy-start.8
  146.5 2.1 copy-start.77
  152.1 2.7 copy-start.73
  152.1 2.7 copy-start.75
  152.1 357.2 %all-reduce.8.cloned.1.call-start = ((), (), s32[]{:S(2)}) async-start(), calls=%async_computation.10 | async-start | bytes 196608 | tf_op jit(solution)/shard_map/psum | solution.py:7
  154.8 719.4 %reduce-scatter.14.cloned.1.call-start = ((), (), s32[]{:S(2)}) async-start(), calls=%async_computation.11 | async-start | bytes 4792320 | tf_op jit(solution)/shard_map/reduce_scatter | solution.py:119
  161.7 1073.3 %reduce-scatter.10.cloned.1.call-start = ((), (), s32[]{:S(2)}) async-start(), calls=%async_computation.7 | async-start | bytes 4792320 | tf_op jit(solution)/shard_map/reduce_scatter | solution.py:117
  168.4 1427.5 %reduce-scatter.12.cloned.1.call-start = ((), (), s32[]{:S(2)}) async-start(), calls=%async_computation.8 | async-start | bytes 4792320 | tf_op jit(solution)/shard_map/reduce_scatter | solution.py:118
  176.0 4.5 copy-start.6
  183.0 10.3 copy-start.7
  (27 other events, 42.1 us)
Sparse Core Ops, SparseCore 0:
  9.7 16.1 all-gather.4
  27.5 14.9 all-gather.6
  121.7 32.9 all-reduce.5
  156.9 13.6 reduce-scatter.5
  172.9 14.0 reduce-scatter.7
  189.3 319.9 all-reduce.7
  512.3 361.8 reduce-scatter.13
  877.1 357.8 reduce-scatter.9
  1238.0 357.8 reduce-scatter.11
